TPU v7x, 32 devices: a whole 2x2x4 slice. The times are simulated.
32 devices in a mesh: dp: 8 (over y, x, core), expert: 4 (over z).
Axes of the slice: x: 2, y: 2, z: 4, core: 2. Of those that a mesh axis runs over, the one named last changes fastest.
Arguments:
- tokens: bfloat16 [12288, 1024], P(('dp', 'expert')), may hold values from -6 to 6
- cotangent: bfloat16 [12288, 1024], P(('dp', 'expert')), may hold values from -6 to 6
- routes: int32 [12288, 8], P(('dp', 'expert')), may hold values from 0 to 15, all different within a row; in each aligned block of 384 rows (0 to 383, 384 to 767, ...) at most 256 rows name the same one
- cont_ids: int32 [32, 128], P(('dp', 'expert')), may hold values from 0 to 1, never falling along the last dimension, each value on 1 to 96 neighbouring positions
- norm_gains: float32 [1024, 2], replicated, may hold values from 0.5 to 1.5
- gains_moment: float32 [1024, 2], P(('dp', 'expert')), may hold values from -192 to 192
- gains_average: float32 [1024, 2], P(('dp', 'expert')), may hold values from 0.5 to 1.5
- heads_in: bfloat16 [1024, 2048], replicated, may hold values from -0.5 to 0.5
- heads_in_master: float32 [1024, 2048], P(('dp', 'expert')), may hold values from -0.625 to 0.625
- heads_in_moment: float32 [1024, 2048], P(('dp', 'expert')), may hold values from -128 to 128
- heads_in_average: float32 [1024, 2048], P(('dp', 'expert')), may hold values from -0.625 to 0.625
- heads_out: bfloat16 [1024, 1024], replicated, may hold values from -1.5 to 1.5
- heads_out_master: float32 [1024, 1024], P(('dp', 'expert')), may hold values from -0.1875 to 0.1875
- heads_out_moment: float32 [1024, 1024], P(('dp', 'expert')), may hold values from -32 to 32
- heads_out_average: float32 [1024, 1024], P(('dp', 'expert')), may hold values from -0.1875 to 0.1875
- router: bfloat16 [1024, 16], replicated, may hold values from -0.09375 to 0.09375
- router_master: float32 [1024, 16], P(('dp', 'expert')), may hold values from -2.5 to 2.5
- router_moment: float32 [1024, 16], P(('dp', 'expert')), may hold values from -128 to 128
- router_average: float32 [1024, 16], P(('dp', 'expert')), may hold values from -2.5 to 2.5
- expert_in: bfloat16 [16, 1024, 1024], P('expert'), may hold values from -0.1875 to 0.1875
- expert_in_master: float32 [16, 1024, 1024], P('expert', 'dp'), may hold values from -0.25 to 0.25
- expert_in_moment: float32 [16, 1024, 1024], P('expert', 'dp'), may hold values from -16 to 16
- expert_in_average: float32 [16, 1024, 1024], P('expert', 'dp'), may hold values from -0.25 to 0.25
- expert_out: bfloat16 [16, 1024, 512], P('expert'), may hold values from -1 to 1
- expert_out_master: float32 [16, 1024, 512], P('expert', 'dp'), may hold values from -0.0546875 to 0.0546875
- expert_out_moment: float32 [16, 1024, 512], P('expert', 'dp'), may hold values from -3.5 to 3.5
- expert_out_average: float32 [16, 1024, 512], P('expert', 'dp'), may hold values from -0.0546875 to 0.0546875
Outputs:
- output: bfloat16 [12288, 1024], P(('dp', 'expert'))
- token_grad: float32 [12288, 1024], P(('dp', 'expert'))
- gains_next: float32 [1024, 2], P(('dp', 'expert'))
- gains_moment_next: float32 [1024, 2], P(('dp', 'expert'))
- gains_average_next: float32 [1024, 2], P(('dp', 'expert'))
- heads_in_next: float32 [1024, 2048], P(('dp', 'expert'))
- heads_in_moment_next: float32 [1024, 2048], P(('dp', 'expert'))
- heads_in_average_next: float32 [1024, 2048], P(('dp', 'expert'))
- heads_out_next: float32 [1024, 1024], P(('dp', 'expert'))
- heads_out_moment_next: float32 [1024, 1024], P(('dp', 'expert'))
- heads_out_average_next: float32 [1024, 1024], P(('dp', 'expert'))
- router_next: float32 [1024, 16], P(('dp', 'expert'))
- router_moment_next: float32 [1024, 16], P(('dp', 'expert'))
- router_average_next: float32 [1024, 16], P(('dp', 'expert'))
- expert_in_next: float32 [16, 1024, 1024], P('expert', 'dp')
- expert_in_moment_next: float32 [16, 1024, 1024], P('expert', 'dp')
- expert_in_average_next: float32 [16, 1024, 1024], P('expert', 'dp')
- expert_out_next: float32 [16, 1024, 512], P('expert', 'dp')
- expert_out_moment_next: float32 [16, 1024, 512], P('expert', 'dp')
- expert_out_average_next: float32 [16, 1024, 512], P('expert', 'dp')
Inputs may be any that keep to these rules, and one draw needn't show every extreme that they name: `routes`: each row names 8 different experts. Among the tokens of one group no expert is named more than 256 times, a bound that some block reaches. `cont_ids`: in each row the numbers never fall; each of the 2 continuations has 1 to 96 tokens.
All inputs are finite; a program needn't handle non-finite values.
Results may differ from a plain program's by a relative error of at most 0.017.
Values may be sent and summed in bfloat16 or wider, within the bound.
A program may use at most 256 MiB of HBM per device.

v0:
```python
import jax
import jax.numpy as jnp
from jax import lax
from jax.sharding import PartitionSpec as P

HEADS = 16
KV_HEADS = 8
HEAD_DIM = 64
EPS = 1e-06
SCALE = 0.015625
THETA = 10000.0
MOMENTUM = 0.9
DECAY = 0.8
RATE = 0.001
HIGHEST = lax.Precision.HIGHEST


def layout(labels_row, prompt_len):
    places = jnp.arange(prompt_len + labels_row.shape[0], dtype=jnp.int32)
    earlier = jnp.sum((labels_row[None, :] < labels_row[:, None]).astype(jnp.int32), axis=1)
    offset = places[prompt_len:] - prompt_len - earlier
    positions = jnp.concatenate([places[:prompt_len], prompt_len + offset]).astype(jnp.float32)
    labels = jnp.concatenate([jnp.full((prompt_len,), -1, jnp.int32), labels_row])
    allowed = (places[None, :] <= places[:, None]) & (
        (places[None, :] < prompt_len) | (labels[None, :] == labels[:, None])
    )
    return (positions, allowed)


def rope_tables(positions):
    middle = HEAD_DIM // 2
    frequency = THETA ** (-2.0 * jnp.arange(middle, dtype=jnp.float32) / HEAD_DIM)
    angles = positions[:, None] * frequency[None, :]
    angles = jnp.concatenate([angles, angles], axis=1)
    return (jnp.cos(angles)[:, None, :], jnp.sin(angles)[:, None, :])


def rotate(values, cosine, sine_table):
    middle = values.shape[-1] // 2
    turned = jnp.concatenate([-values[..., middle:], values[..., :middle]], axis=-1)
    return values * cosine + turned * sine_table


def unrotate(gradient, cosine, sine_table):
    middle = gradient.shape[-1] // 2
    shifted = gradient * sine_table
    return gradient * cosine + jnp.concatenate(
        [shifted[..., middle:], -shifted[..., :middle]], axis=-1
    )


def masked_scores(queries, key_rows, allowed):
    products = (
        jnp.einsum("qkgd,pkd->kgqp", queries, key_rows, preferred_element_type=jnp.float32) * SCALE
    )
    return jnp.where(allowed[None, None], products, -1e30)


def rms_parts(values, gain):
    factor = lax.rsqrt(jnp.mean(values * values, axis=-1, keepdims=True) + EPS)
    return (values * factor * gain, factor)


def rms_back(incoming, values, factor, gain):
    normed = values * factor
    gain_grad = jnp.sum(incoming * normed, axis=0)
    weighted = incoming * gain
    input_grad = factor * (weighted - normed * jnp.mean(weighted * normed, axis=-1, keepdims=True))
    return (input_grad, gain_grad)


def bank_total(values, scales, bank_hot):
    partial_value = jnp.einsum(
        "tk,tkp,tkd->tpd", scales, bank_hot, values.astype(jnp.float32), precision=HIGHEST
    )
    return jnp.sum(partial_value.astype(jnp.bfloat16).astype(jnp.float32), axis=1)


def update(gradient, master, moment, average):
    moment_next = MOMENTUM * moment + gradient
    master_next = master - RATE * (gradient + MOMENTUM * moment_next)
    return (master_next, moment_next, DECAY * average + (1.0 - DECAY) * master_next)


def body(
    tokens,
    cotangent,
    routes,
    cont_ids,
    norm_gains,
    gains_moment,
    gains_average,
    heads_in,
    heads_in_master,
    heads_in_moment,
    heads_in_average,
    heads_out,
    heads_out_master,
    heads_out_moment,
    heads_out_average,
    router,
    router_master,
    router_moment,
    router_average,
    expert_in,
    expert_in_master,
    expert_in_moment,
    expert_in_average,
    expert_out,
    expert_out_master,
    expert_out_moment,
    expert_out_average,
):
    token_count, model_width = tokens.shape
    fanout = routes.shape[1]
    local_experts = expert_in.shape[0]
    peer_count = lax.axis_size("expert")
    experts = local_experts * peer_count
    capacity = 4 * token_count * fanout // (3 * experts)
    ff_width = expert_out.shape[2]
    group_size = HEADS // KV_HEADS
    query_end = HEADS * HEAD_DIM
    key_end = query_end + KV_HEADS * HEAD_DIM
    token_rows = tokens.astype(jnp.float32)
    normed_one, factor_one = rms_parts(token_rows, norm_gains[:, 0])
    first_in = normed_one.astype(jnp.bfloat16)
    projected = jnp.dot(first_in, heads_in, preferred_element_type=jnp.float32)
    positions, allowed = layout(cont_ids[0], token_count - cont_ids.shape[1])
    cosine, sine_table = rope_tables(positions)
    queries = rotate(
        projected[:, :query_end].reshape(token_count, HEADS, HEAD_DIM), cosine, sine_table
    )
    queries = queries.astype(jnp.bfloat16).reshape(token_count, KV_HEADS, group_size, HEAD_DIM)
    key_rows = rotate(
        projected[:, query_end:key_end].reshape(token_count, KV_HEADS, HEAD_DIM), cosine, sine_table
    ).astype(jnp.bfloat16)
    value_rows = (
        projected[:, key_end:].reshape(token_count, KV_HEADS, HEAD_DIM).astype(jnp.bfloat16)
    )
    scores = masked_scores(queries, key_rows, allowed)
    row_peak = jnp.max(scores, axis=-1, keepdims=True)
    log_total = row_peak + jnp.log(jnp.sum(jnp.exp(scores - row_peak), axis=-1, keepdims=True))
    weights = jnp.exp(scores - log_total).astype(jnp.bfloat16)
    attended = jnp.einsum("kgqp,pkd->qkgd", weights, value_rows, preferred_element_type=jnp.float32)
    attended = attended.reshape(token_count, query_end).astype(jnp.bfloat16)
    branch = jnp.einsum("th,dh->td", attended, heads_out, preferred_element_type=jnp.float32)
    hidden = token_rows + branch
    normed_two, factor_two = rms_parts(hidden, norm_gains[:, 1])
    second_in = normed_two.astype(jnp.bfloat16)
    logits = jnp.dot(second_in, router, preferred_element_type=jnp.float32)
    gate_probs = jax.nn.softmax(jnp.take_along_axis(logits, routes, axis=1), axis=-1)
    incoming = cotangent.astype(jnp.float32)
    matches = (routes[:, :, None] == jnp.arange(experts, dtype=jnp.int32)[None, None, :]).astype(
        jnp.int32
    )
    counts = jnp.sum(matches, axis=1)
    before = jnp.cumsum(counts, axis=0) - counts
    flat_rows = routes * capacity + jnp.take_along_axis(before, routes, axis=1)
    token_ids = jnp.broadcast_to(jnp.arange(token_count, dtype=jnp.int32)[:, None], routes.shape)
    slot_tokens = (
        jnp.full((experts * capacity,), token_count, jnp.int32)
        .at[flat_rows.reshape(-1)]
        .set(token_ids.reshape(-1))
    )
    slot_picks = (
        jnp.full((experts * capacity,), token_count * fanout, jnp.int32)
        .at[flat_rows.reshape(-1)]
        .set(jnp.arange(token_count * fanout, dtype=jnp.int32))
    )
    slot_gates = jnp.take(gate_probs.reshape(-1), slot_picks, axis=0, mode="fill", fill_value=0.0)
    peer_ids = jnp.arange(peer_count, dtype=jnp.int32)
    owners = routes // local_experts
    bank_hot = (owners[:, :, None] == peer_ids[None, None, :]).astype(jnp.float32)
    outgoing = jnp.take(second_in, slot_tokens, axis=0, mode="fill", fill_value=0).reshape(
        experts, capacity, model_width
    )
    inputs = lax.all_to_all(outgoing, "expert", split_axis=0, concat_axis=1, tiled=True)
    gate_up = jnp.einsum("erd,edf->erf", inputs, expert_in, preferred_element_type=jnp.float32)
    gate_part = gate_up[..., :ff_width]
    up_part = gate_up[..., ff_width:]
    activated = (jax.nn.silu(gate_part) * up_part).astype(jnp.bfloat16)
    result = jnp.einsum(
        "erf,edf->erd", activated, expert_out, preferred_element_type=jnp.float32
    ).astype(jnp.bfloat16)
    returned = lax.all_to_all(result, "expert", split_axis=1, concat_axis=0, tiled=True).reshape(
        experts * capacity, model_width
    )
    chosen = jnp.take(returned, flat_rows.reshape(-1), axis=0).reshape(
        token_count, fanout, model_width
    )
    mixture = bank_total(chosen, gate_probs, bank_hot)
    grad_gates = jnp.einsum("td,tkd->tk", cotangent, chosen, preferred_element_type=jnp.float32)
    outgoing_grads = (
        slot_gates[:, None] * jnp.take(cotangent, slot_tokens, axis=0, mode="fill", fill_value=0)
    ).astype(jnp.bfloat16)
    grad_result = lax.all_to_all(
        outgoing_grads.reshape(experts, capacity, model_width),
        "expert",
        split_axis=0,
        concat_axis=1,
        tiled=True,
    )
    output = (hidden + mixture).astype(jnp.bfloat16)
    grad_activated = jnp.einsum(
        "erd,edf->erf", grad_result, expert_out, preferred_element_type=jnp.float32
    )
    sigmoid_gate = jax.nn.sigmoid(gate_part)
    grad_gate_part = (
        grad_activated * up_part * sigmoid_gate * (1.0 + gate_part * (1.0 - sigmoid_gate))
    )
    grad_up_part = grad_activated * (gate_part * sigmoid_gate)
    grad_gate_up = jnp.concatenate([grad_gate_part, grad_up_part], axis=-1).astype(jnp.bfloat16)
    grad_expert_out = jnp.einsum(
        "erd,erf->edf", grad_result, activated, preferred_element_type=jnp.float32
    )
    grad_expert_in = jnp.einsum(
        "erd,erf->edf", inputs, grad_gate_up, preferred_element_type=jnp.float32
    )
    grad_inputs = jnp.einsum(
        "erf,edf->erd", grad_gate_up, expert_in, preferred_element_type=jnp.float32
    ).astype(jnp.bfloat16)
    returned_grads = lax.all_to_all(
        grad_inputs, "expert", split_axis=1, concat_axis=0, tiled=True
    ).reshape(experts * capacity, model_width)
    gathered_grads = jnp.take(returned_grads, flat_rows.reshape(-1), axis=0).reshape(
        token_count, fanout, model_width
    )
    grad_second = bank_total(gathered_grads, jnp.ones((token_count, fanout), jnp.float32), bank_hot)
    weighted_sum = jnp.sum(gate_probs * grad_gates, axis=1, keepdims=True)
    grad_picked = gate_probs * (grad_gates - weighted_sum)
    grad_logits = jnp.einsum(
        "tk,tke->te", grad_picked, matches.astype(jnp.float32), precision=HIGHEST
    )
    grad_router = jnp.dot(second_in.astype(jnp.float32).T, grad_logits, precision=HIGHEST)
    grad_second = grad_second + jnp.dot(
        grad_logits, router.astype(jnp.float32).T, precision=HIGHEST
    )
    grad_hidden_norm, grad_gain_two = rms_back(grad_second, hidden, factor_two, norm_gains[:, 1])
    grad_hidden = incoming + grad_hidden_norm
    grad_branch = grad_hidden.astype(jnp.bfloat16)
    grad_heads_out = jnp.einsum(
        "td,th->dh", grad_branch, attended, preferred_element_type=jnp.float32
    )
    grad_attended = jnp.dot(grad_branch, heads_out, preferred_element_type=jnp.float32).astype(
        jnp.bfloat16
    )
    grad_attended = grad_attended.reshape(token_count, KV_HEADS, group_size, HEAD_DIM)
    weight_full = jnp.exp(masked_scores(queries, key_rows, allowed) - log_total)
    grad_weights = jnp.einsum(
        "qkgd,pkd->kgqp", grad_attended, value_rows, preferred_element_type=jnp.float32
    )
    spread = jnp.sum(weight_full * grad_weights, axis=-1, keepdims=True)
    grad_scores = (weight_full * (grad_weights - spread)).astype(jnp.bfloat16)
    grad_queries = (
        jnp.einsum("kgqp,pkd->qkgd", grad_scores, key_rows, preferred_element_type=jnp.float32)
        * SCALE
    )
    grad_keys = (
        jnp.einsum("kgqp,qkgd->pkd", grad_scores, queries, preferred_element_type=jnp.float32)
        * SCALE
    )
    grad_values = jnp.einsum(
        "kgqp,qkgd->pkd",
        weight_full.astype(jnp.bfloat16),
        grad_attended,
        preferred_element_type=jnp.float32,
    )
    grad_projected = jnp.concatenate(
        [
            unrotate(
                grad_queries.reshape(token_count, HEADS, HEAD_DIM), cosine, sine_table
            ).reshape(token_count, query_end),
            unrotate(grad_keys, cosine, sine_table).reshape(token_count, KV_HEADS * HEAD_DIM),
            grad_values.reshape(token_count, KV_HEADS * HEAD_DIM),
        ],
        axis=1,
    ).astype(jnp.bfloat16)
    grad_heads_in = jnp.einsum(
        "td,tc->dc", first_in, grad_projected, preferred_element_type=jnp.float32
    )
    grad_first = jnp.einsum(
        "tc,dc->td", grad_projected, heads_in, preferred_element_type=jnp.float32
    )
    grad_tokens_norm, grad_gain_one = rms_back(grad_first, token_rows, factor_one, norm_gains[:, 0])
    token_grad = grad_hidden + grad_tokens_norm
    grad_gains = jnp.stack([grad_gain_one, grad_gain_two], axis=1)
    summed = (
        lax.psum_scatter(grad_heads_in, ("dp", "expert"), scatter_dimension=0, tiled=True),
        lax.psum_scatter(grad_heads_out, ("dp", "expert"), scatter_dimension=0, tiled=True),
        lax.psum_scatter(grad_router, ("dp", "expert"), scatter_dimension=0, tiled=True),
        lax.psum_scatter(grad_gains, ("dp", "expert"), scatter_dimension=0, tiled=True),
    )
    expert_sums = (
        lax.psum_scatter(
            grad_expert_in.astype(jnp.bfloat16), "dp", scatter_dimension=1, tiled=True
        ).astype(jnp.float32),
        lax.psum_scatter(
            grad_expert_out.astype(jnp.bfloat16), "dp", scatter_dimension=1, tiled=True
        ).astype(jnp.float32),
    )
    shard_rows = model_width // lax.axis_size(("dp", "expert"))
    gains_share = lax.dynamic_slice_in_dim(
        norm_gains, lax.axis_index(("dp", "expert")) * shard_rows, shard_rows, 0
    )
    gains_new = update(summed[3], gains_share, gains_moment, gains_average)
    inproj_new = update(summed[0], heads_in_master, heads_in_moment, heads_in_average)
    outproj_new = update(summed[1], heads_out_master, heads_out_moment, heads_out_average)
    router_new = update(summed[2], router_master, router_moment, router_average)
    upper_new = update(expert_sums[0], expert_in_master, expert_in_moment, expert_in_average)
    lower_new = update(expert_sums[1], expert_out_master, expert_out_moment, expert_out_average)
    return (
        output,
        token_grad,
        gains_new[0],
        gains_new[1],
        gains_new[2],
        inproj_new[0],
        inproj_new[1],
        inproj_new[2],
        outproj_new[0],
        outproj_new[1],
        outproj_new[2],
        router_new[0],
        router_new[1],
        router_new[2],
        upper_new[0],
        upper_new[1],
        upper_new[2],
        lower_new[0],
        lower_new[1],
        lower_new[2],
    )


def solution(mesh):
    return jax.shard_map(
        body,
        mesh=mesh,
        in_specs=(
            P(("dp", "expert"), None),
            P(("dp", "expert"), None),
            P(("dp", "expert"), None),
            P(("dp", "expert"), None),
            P(),
            P(("dp", "expert"), None),
            P(("dp", "expert"), None),
            P(),
            P(("dp", "expert"), None),
            P(("dp", "expert"), None),
            P(("dp", "expert"), None),
            P(),
            P(("dp", "expert"), None),
            P(("dp", "expert"), None),
            P(("dp", "expert"), None),
            P(),
            P(("dp", "expert"), None),
            P(("dp", "expert"), None),
            P(("dp", "expert"), None),
            P("expert", None, None),
            P("expert", "dp", None),
            P("expert", "dp", None),
            P("expert", "dp", None),
            P("expert", None, None),
            P("expert", "dp", None),
            P("expert", "dp", None),
            P("expert", "dp", None),
        ),
        out_specs=(
            P(("dp", "expert"), None),
            P(("dp", "expert"), None),
            P(("dp", "expert"), None),
            P(("dp", "expert"), None),
            P(("dp", "expert"), None),
            P(("dp", "expert"), None),
            P(("dp", "expert"), None),
            P(("dp", "expert"), None),
            P(("dp", "expert"), None),
            P(("dp", "expert"), None),
            P(("dp", "expert"), None),
            P(("dp", "expert"), None),
            P(("dp", "expert"), None),
            P(("dp", "expert"), None),
            P("expert", "dp", None),
            P("expert", "dp", None),
            P("expert", "dp", None),
            P("expert", "dp", None),
            P("expert", "dp", None),
            P("expert", "dp", None),
        ),
        check_vma=False,
    )
```

profile of v0, /device:TPU:0, one launch (start us, length us, event | category | flops | bytes accessed | tf_op | source)
XLA Modules:
  0.0 1631.6 jit_solution(6618232595936007298)
XLA Ops:
  9.5 4.3 fusion.56
  17.6 3.0 copy.184
  20.6 2.6 slice_negate_fusion.1
  24.4 1.5 copy.183
  29.9 2.3 fusion.33
  32.3 1.6 fusion.13
  33.9 1.9 exponential_reduce_fusion
  35.8 1.7 copy-done.2
  37.5 2.4 convolution_convert_fusion.5
  39.9 2.2 multiply_reduce_fusion.2
  42.7 1.6 multiply_convert_fusion.4
  44.7 25.2 %gather_fusion.1 = f32[3072]{0:T(1024)S(1)} fusion(f32[384,16]{0,1:T(8,128)S(1)} %fusion.96, s32[3072]{0:T(1024)S(1)} %reshape.416), kind=kCustom, calls=%fused_computation.5 | custom fusion | bytes 49152 | tf_op jit(solution)/shard_map/jit(take_along_axis)/gather | solution.py:151
  72.1 20.2 %gather_fusion.2 = s32[3072]{0:T(1024)S(1)} fusion(s32[384,16]{1,0:T(8,128)S(1)} %bitcast_subtract_fusion.1, s32[3072]{0:T(1024)S(1)} %reshape.416), kind=kCustom, calls=%fused_computation.6 | custom fusion | bytes 49152 | tf_op jit(solution)/shard_map/jit(take_along_axis)/gather | solution.py:158
  93.5 11.8 scatter_custom_fusion
  105.4 18.3 %gather_fusion.3 = bf16[4096,1024]{1,0:T(8,128)(2,1)} fusion(bf16[384,1024]{1,0:T(8,128)(2,1)S(1)} %multiply_convert_fusion.4, s32[4096]{0:T(1024)S(1)} %fusion.65), kind=kCustom, calls=%fused_computation.clone | custom fusion | bytes 16793600 | tf_op jit(solution)/shard_map/jit(_take)/gather | solution.py:174
  123.7 4.4 broadcast_select_fusion
  128.1 189.2 %all_to_all.66 = bf16[16,256,1024]{2,1,0:T(8,128)(2,1)} all-to-all(bf16[16,256,1024]{2,1,0:T(8,128)(2,1)S(1)} %bitcast.173), channel_id=1, replica_groups=mesh['dp'=8,'expert'=4] {'expert'}, dimensions={0} | all-to-all | bytes 16777216 | tf_op jit(solution)/shard_map/all_to_all | solution.py:177
  317.3 8.0 copy.198
  325.3 17.0 %fusion.97 = f32[4,1024,1024]{1,2,0:T(8,128)} fusion(bf16[4,1024,1024]{2,1,0:T(8,128)(2,1)} %bitcast.178, bf16[4,1024,1024]{2,1,0:T(8,128)(2,1)} %param.50), kind=kOutput, calls=%fused_computation.204 | convolution fusion | flops 8589934592 | bytes 33554432 | tf_op jit(solution)/shard_map/erd,edf->erf/dot_general | solution.py:178
  342.3 8.5 multiply_convert_fusion.3
  350.9 11.6 convolution_convert_fusion.2
  362.5 22.5 %copy.201 = bf16[4,1024,1024]{2,0,1:T(4,128)(2,1)} copy(bf16[4,1024,1024]{2,1,0:T(8,128)(2,1)} %convolution_convert_fusion.2) | data formatting | bytes 16777216 | tf_op jit(solution)/shard_map/convert_element_type | solution.py:184
  385.0 5.6 all-to-all-start.1
  390.8 22.1 %gather_fusion.5 = bf16[4096,1024]{1,0:T(8,128)(2,1)} fusion(bf16[384,1024]{1,0:T(8,128)(2,1)} %param.32, s32[4096]{0:T(1024)S(1)} %fusion.65), kind=kCustom, calls=%fused_computation.2.clone | custom fusion | bytes 16793600 | tf_op jit(solution)/shard_map/jit(_take)/gather | solution.py:194
  412.9 11.8 scatter_custom_fusion.1
  424.8 148.0 %all-to-all-done.1 = bf16[4,1024,1024]{2,0,1:T(4,128)(2,1)} async-done(((bf16[4,1024,1024]{2,0,1:T(4,128)(2,1)}), bf16[4,1024,1024]{2,0,1:T(4,128)(2,1)}, u32[]{:S(2)}, u32[]{:S(2)}) %all-to-all-start.1) | async-done | bytes 8388640 | tf_op jit(solution)/shard_map/all_to_all | solution.py:185
  572.8 9.8 copy.202
  582.6 20.4 %gather_fusion.4 = bf16[3072,1024]{1,0:T(8,128)(2,1)} fusion(bf16[4096,1024]{1,0:T(8,128)(2,1)} %bitcast.168, s32[3072]{0:T(1024)S(1)} %fusion.72), kind=kCustom, calls=%fused_computation.1.clone | custom fusion | bytes 12595200 | tf_op jit(solution)/shard_map/jit(_take)/gather | solution.py:188
  603.0 7.6 fusion.7
  611.0 23.0 %gather_fusion = f32[4096]{0:T(1024)S(1)} fusion(f32[3072]{0:T(1024)S(1)} %div.58, s32[4096]{0:T(1024)S(1)} %fusion.64), kind=kCustom, calls=%fused_computation.4 | custom fusion | bytes 49152 | tf_op jit(solution)/shard_map/jit(_take)/gather | solution.py:170
  634.1 7.8 multiply_convert_fusion
  641.9 5.6 all-to-all-start.2
  647.6 1.7 fusion.98
  649.3 186.8 %all-to-all-done.2 = bf16[16,256,1024]{2,1,0:T(8,128)(2,1)} async-done(((bf16[16,256,1024]{2,1,0:T(8,128)(2,1)}), bf16[16,256,1024]{2,1,0:T(8,128)(2,1)}, u32[]{:S(2)}, u32[]{:S(2)}) %all-to-all-start.2) | async-done | bytes 8388640 | tf_op jit(solution)/shard_map/all_to_all | solution.py:196
  836.1 8.1 copy.204
  844.2 15.5 multiply_convert_fusion.2
  859.7 16.5 %convolution_convert_fusion.1 = bf16[4,1024,1024]{2,1,0:T(8,128)(2,1)} fusion(bf16[4,1024,1024]{2,1,0:T(8,128)(2,1)} %param.50, bf16[4,1024,512]{1,2,0:T(8,128)(2,1)} %get-tuple-element.49, bf16[4,1024,512]{1,2,0:T(8,128)(2,1)} %get-tuple-element.48), kind=kOutput, calls=%fused_computation.27 | convolution fusion | flops 8610906112 | bytes 25165824 | tf_op jit(solution)/shard_map/erf,edf->erd/dot_general | solution.py:219
  876.1 12.1 copy.207
  888.3 5.6 all-to-all-start.3
  894.4 11.8 convolution_convert_fusion.3
  906.2 16.3 %convolution_convert_fusion = bf16[4,1024,1024]{2,1,0:T(8,128)(2,1)} fusion(bf16[4,1024,1024]{2,1,0:T(8,128)(2,1)} %bitcast.179, bf16[4,1024,512]{1,2,0:T(8,128)(2,1)} %get-tuple-element.49, bf16[4,1024,512]{1,2,0:T(8,128)(2,1)} %get-tuple-element.48), kind=kOutput, calls=%fused_computation.26 | convolution fusion | flops 8610906112 | bytes 25165824 | tf_op jit(solution)/shard_map/erd,erf->edf/dot_general | solution.py:216
  923.4 11.6 convert_reduce_fusion.1
  935.0 141.3 %all-to-all-done.3 = bf16[4,1024,1024]{2,0,1:T(4,128)(2,1)} async-done(((bf16[4,1024,1024]{2,0,1:T(4,128)(2,1)}), bf16[4,1024,1024]{2,0,1:T(4,128)(2,1)}, u32[]{:S(2)}, u32[]{:S(2)}) %all-to-all-start.3) | async-done | bytes 8388640 | tf_op jit(solution)/shard_map/all_to_all | solution.py:222
  1076.3 9.7 copy.208
  1086.1 20.4 %gather_fusion.6 = bf16[3072,1024]{1,0:T(8,128)(2,1)} fusion(bf16[4096,1024]{1,0:T(8,128)(2,1)} %bitcast.167, s32[3072]{0:T(1024)S(1)} %fusion.72), kind=kCustom, calls=%fused_computation.3.clone | custom fusion | bytes 12595200 | tf_op jit(solution)/shard_map/jit(_take)/gather | solution.py:225
  1106.5 7.2 convert_reduce_fusion
  1117.9 1.9 convolution_convert_fusion.4
  1119.8 1.5 copy.209
  1121.3 7.9 fusion
  1129.2 11.4 fusion.2
  1140.7 3.4 convolution_multiply_fusion
  1145.8 1.5 broadcast_multiply_fusion
  1149.0 2.4 fusion.37
  1151.4 3.2 fusion.30
  1155.8 4.9 fusion.48
  1161.1 7.1 fusion.44
  1169.7 4.2 multiply_add_fusion.2
  1173.9 1.6 fusion.29
  1175.6 7.1 multiply_add_fusion
  1182.8 106.7 %reduce-scatter.19.cloned.1.call-done = f32[32,2]{1,0:T(8,128)} async-done(((f32[1024,2]{1,0:T(8,128)}), f32[32,2]{1,0:T(8,128)}) %reduce-scatter.19.cloned.1.call-update) | async-done | bytes 272
  1291.6 144.2 %reduce-scatter.13.cloned.1.call-done = f32[32,1024]{1,0:T(8,128)} async-done(((f32[1024,1024]{1,0:T(8,128)}), f32[32,1024]{1,0:T(8,128)}) %reduce-scatter.13.cloned.1.call-update) | async-done | bytes 131088 | tf_op jit(solution)/shard_map/reduce_scatter | solution.py:289
  1435.8 1.7 multiply_add_fusion.5
  1437.5 184.9 %reduce-scatter.11.cloned.1.call-done = f32[32,2048]{1,0:T(8,128)} async-done(((f32[1024,2048]{1,0:T(8,128)}), f32[32,2048]{1,0:T(8,128)}) %reduce-scatter.11.cloned.1.call-update) | async-done | bytes 262160 | tf_op jit(solution)/shard_map/reduce_scatter | solution.py:288
  1622.4 1.9 multiply_add_fusion.3
  (227 shorter events, 29.9 us)
Async XLA Ops:
  7.2 32.7 %copy-start = (bf16[1024,1024]{1,0:T(8,128)(2,1)S(1)}, bf16[1024,1024]{1,0:T(8,128)(2,1)}, u32[]{:S(2)}) copy-start(bf16[1024,1024]{1,0:T(8,128)(2,1)} %param.42) | copy-start | bytes 6291460
  8.1 5.7 copy-start.34
  8.1 34.3 %copy-start.46 = (f32[1024,1]{0,1:T(1,128)}, f32[1024,1]{0,1:T(1,128)S(1)}, u32[]{:S(2)}) copy-start(f32[1024,1]{0,1:T(1,128)S(1)} %get-tuple-element.66) | copy-start | bytes 12292
  9.5 4.3 copy-start.48
  13.8 2.3 copy-start.30
  15.1 8.1 copy-start.59
  24.4 7.8 copy-start.17
  24.4 7.8 copy-start.21
  28.6 7.2 copy-start.12
  29.9 3.9 copy-start.10
  32.2 1.6 copy-start.8
  33.8 3.7 copy-start.2
  33.9 3.6 copy-start.23
  35.8 4.1 copy-start.36
  37.5 2.4 copy-start.6
  39.9 2.2 copy-start.26
  39.9 4.4 copy-start.40
  44.6 26.0 %copy-start.45 = (s32[16,3,128]{2,0,1:T(8,128)S(1)}, s32[16,3,128]{2,0,1:T(8,128)}, u32[]{:S(2)}) copy-start(s32[16,3,128]{2,0,1:T(8,128)} %copy_bitcast_fusion) | copy-start | bytes 73732
  44.6 27.4 %copy-start.25 = (s32[384,16]{1,0:T(8,128)S(1)}, s32[384,16]{1,0:T(8,128)}, u32[]{:S(2)}) copy-start(s32[384,16]{1,0:T(8,128)} %copy.194) | copy-start | bytes 73732
  70.1 1.8 copy-start.38
  385.0 187.8 %all-to-all-start.1 = ((bf16[4,1024,1024]{2,0,1:T(4,128)(2,1)}), bf16[4,1024,1024]{2,0,1:T(4,128)(2,1)}, u32[]{:S(2)}, u32[]{:S(2)}) async-start(bf16[4,1024,1024]{2,0,1:T(4,128)(2,1)} %copy.201), calls=%async_computation.1 | async-start | bytes 16777216 | tf_op jit(solution)/shard_map/all_to_all | solution.py:185
  390.7 34.0 %copy-start.39 = (f32[384,8]{0,1:T(8,128)S(1)}, f32[384,8]{0,1:T(8,128)}, u32[]{:S(2)}) copy-start(f32[384,8]{0,1:T(8,128)} %copy-done.38) | copy-start | bytes 36868
  390.8 34.0 %copy-start.53 = (f32[384]{0:T(512)S(1)}, f32[384]{0:T(512)}, u32[]{:S(2)}) copy-start(f32[384]{0:T(512)} %get-tuple-element.46) | copy-start | bytes 4612
  641.9 194.2 %all-to-all-start.2 = ((bf16[16,256,1024]{2,1,0:T(8,128)(2,1)}), bf16[16,256,1024]{2,1,0:T(8,128)(2,1)}, u32[]{:S(2)}, u32[]{:S(2)}) async-start(bf16[16,256,1024]{2,1,0:T(8,128)(2,1)} %bitcast.174), calls=%async_computation.2 | async-start | bytes 16777216 | tf_op jit(solution)/shard_map/all_to_all | solution.py:196
  647.5 520.8 %reduce-scatter.21.cloned.1.call-start = ((), (), s32[]{:S(2)}) async-start(), calls=%async_computation.15 | async-start | bytes 540672
  888.3 188.1 %all-to-all-start.3 = ((bf16[4,1024,1024]{2,0,1:T(4,128)(2,1)}), bf16[4,1024,1024]{2,0,1:T(4,128)(2,1)}, u32[]{:S(2)}, u32[]{:S(2)}) async-start(bf16[4,1024,1024]{2,0,1:T(4,128)(2,1)} %copy.207), calls=%async_computation.3 | async-start | bytes 16777216 | tf_op jit(solution)/shard_map/all_to_all | solution.py:222
  893.9 275.8 %reduce-scatter.17.cloned.1.call-start = ((), (), s32[]{:S(2)}) async-start(), calls=%async_computation.13 | async-start | bytes 4718592 | tf_op jit(solution)/shard_map/reduce_scatter | solution.py:297
  906.2 269.4 %reduce-scatter.15.cloned.1.call-start = ((), (), s32[]{:S(2)}) async-start(), calls=%async_computation.12 | async-start | bytes 9437184 | tf_op jit(solution)/shard_map/reduce_scatter | solution.py:294
  922.6 366.9 %reduce-scatter.19.cloned.1.call-start = ((), (), s32[]{:S(2)}) async-start(), calls=%async_computation.14 | async-start | bytes 540672
  1106.5 7.3 copy-start.5
  1106.5 7.3 copy-start.41
  1106.5 7.3 copy-start.47
  1106.5 7.3 copy-start.52
  1113.8 1.6 copy-start.20
  1117.9 3.4 copy-start.13
  1117.9 3.4 copy-start.24
  1117.9 3.4 copy-start.37
  1121.3 7.9 copy-start.14
  1129.2 11.4 copy-start.11
  1140.7 3.5 copy-start.18
  1140.7 4.6 slice-start.3
  1144.2 3.4 slice-start
  1144.5 3.9 slice-start.1
  1145.2 6.1 copy-start.16
  1145.8 1.7 copy-start.28
  1145.8 2.9 slice-start.2
  1145.8 3.1 copy-start.15
  1149.0 2.4 copy-start.7
  1149.0 2.4 copy-start.35
  1149.0 2.5 copy-start.49
  1149.0 2.5 copy-start.60
  1151.4 3.3 copy-start.29
  1155.7 280.0 %reduce-scatter.13.cloned.1.call-start = ((), (), s32[]{:S(2)}) async-start(), calls=%async_computation.11 | async-start | bytes 4325376 | tf_op jit(solution)/shard_map/reduce_scatter | solution.py:289
  1160.7 461.6 %reduce-scatter.11.cloned.1.call-start = ((), (), s32[]{:S(2)}) async-start(), calls=%async_computation.10 | async-start | bytes 8650752 | tf_op jit(solution)/shard_map/reduce_scatter | solution.py:288
  1169.7 4.2 copy-start.4
  1169.7 4.2 copy-start.19
  1175.5 114.7 %copy-start.57 = (f32[32,2]{0,1:T(2,128)S(1)}, f32[32,2]{0,1:T(2,128)}, u32[]{:S(2)}) copy-start(f32[32,2]{0,1:T(2,128)} %param.37) | copy-start | bytes 772
  1175.5 114.7 %copy-start.58 = (f32[32,2]{0,1:T(2,128)S(1)}, f32[32,2]{0,1:T(2,128)}, u32[]{:S(2)}) copy-start(f32[32,2]{0,1:T(2,128)} %param.36) | copy-start | bytes 772
  1175.5 260.2 %copy-start.42 = (f32[32,1024]{1,0:T(8,128)S(1)}, f32[32,1024]{1,0:T(8,128)}, u32[]{:S(2)}) copy-start(f32[32,1024]{1,0:T(8,128)} %param.45) | copy-start | bytes 393220
  1175.5 260.2 %copy-start.43 = (f32[32,1024]{1,0:T(8,128)S(1)}, f32[32,1024]{1,0:T(8,128)}, u32[]{:S(2)}) copy-start(f32[32,1024]{1,0:T(8,128)} %param.43) | copy-start | bytes 393220
  1175.5 260.2 %copy-start.44 = (f32[32,1024]{1,0:T(8,128)S(1)}, f32[32,1024]{1,0:T(8,128)}, u32[]{:S(2)}) copy-start(f32[32,1024]{1,0:T(8,128)} %param.44) | copy-start | bytes 393220
  1175.6 446.8 %copy-start.31 = (f32[32,2048]{1,0:T(8,128)S(1)}, f32[32,2048]{1,0:T(8,128)}, u32[]{:S(2)}) copy-start(f32[32,2048]{1,0:T(8,128)} %param.41) | copy-start | bytes 786436
  1175.6 446.8 %copy-start.32 = (f32[32,2048]{1,0:T(8,128)S(1)}, f32[32,2048]{1,0:T(8,128)}, u32[]{:S(2)}) copy-start(f32[32,2048]{1,0:T(8,128)} %param.39) | copy-start | bytes 786436
  1175.6 446.8 %copy-start.33 = (f32[32,2048]{1,0:T(8,128)S(1)}, f32[32,2048]{1,0:T(8,128)}, u32[]{:S(2)}) copy-start(f32[32,2048]{1,0:T(8,128)} %param.40) | copy-start | bytes 786436
  (11 other events, 10.9 us)
Sparse Core Ops, SparseCore 0:
  651.1 243.6 reduce-scatter.20
  906.3 52.8 reduce-scatter.16
  962.6 71.2 reduce-scatter.14
  1155.9 133.5 reduce-scatter.18
  1291.6 144.1 reduce-scatter.12
  1437.9 184.4 reduce-scatter.10
where the time goes:
time: 1640 us; the launch traced here: 1630 us
  waiting for transfers between devices  912 us (56%)
  local copies, waits for them, and re-layouts  267 us (16%)
  blocking collectives  189 us (12%)
  matrix products  161 us (10%)
  other arithmetic  68.7 us (4%)
  starting transfers between devices  17.9 us (1%)
    all_to_all x1, blocking collectives, body(): lax.all_to_all(outgoing, 'expert', split_axis=0, concat_axis=1, tiled=True)  189 us
    all_to_all x1, waiting for transfers between devices, body(): lax.all_to_all(outgoing_grads.reshape(experts, capacity, model_width), 'e...  187 us
    reduce_scatter x1, waiting for transfers between devices, body(): lax.psum_scatter(grad_heads_in, ('dp', 'expert'), scatter_dimension=0, ti...  185 us
    all_to_all x1, waiting for transfers between devices, body(): lax.all_to_all(result, 'expert', split_axis=1, concat_axis=0, tiled=True)  148 us
    reduce_scatter x1, waiting for transfers between devices, body(): lax.psum_scatter(grad_heads_out, ('dp', 'expert'), scatter_dimension=0, t...  144 us
    all_to_all x1, waiting for transfers between devices, body(): lax.all_to_all(grad_inputs, 'expert', split_axis=1, concat_axis=0, tiled=...  141 us
    unnamed x8, waiting for transfers between devices  107 us
  transfers between devices with their start and end apart: 9, of which 6 were waited for; matrix products, arithmetic and copies ran while one was open for 14% of the time, Pallas kernels for 0%

commit v1 on v0

--- a/solution.py
+++ b/solution.py
@@ -13,6 +13,29 @@
 DECAY = 0.8
 RATE = 0.001
 HIGHEST = lax.Precision.HIGHEST
+
+
+def in_blocks(x, dim, size):
+    lengths = x.shape
+    pieces = x.reshape(*lengths[:dim], size, lengths[dim] // size, *lengths[dim + 1 :])
+    return jnp.moveaxis(pieces, dim, 0)
+
+
+def laid_out(pieces, dim):
+    pieces = jnp.moveaxis(pieces, 0, dim)
+    lengths = pieces.shape
+    return pieces.reshape(*lengths[:dim], lengths[dim] * lengths[dim + 1], *lengths[dim + 2 :])
+
+
+def pairwise_exchange(x, axis, split_dim, concat_dim):
+    size, position = (lax.axis_size(axis), lax.axis_index(axis))
+    blocks = in_blocks(x, split_dim, size)
+    gathered = [blocks[position]]
+    for step in range(1, size):
+        sent = blocks[position ^ step]
+        gathered.append(lax.ppermute(sent, axis, [(i, i ^ step) for i in range(size)]))
+    blocks = jnp.stack(gathered)[position ^ jnp.arange(size)]
+    return laid_out(blocks, concat_dim)
 
 
 def layout(labels_row, prompt_len):
@@ -219,9 +242,9 @@
     grad_inputs = jnp.einsum(
         "erf,edf->erd", grad_gate_up, expert_in, preferred_element_type=jnp.float32
     ).astype(jnp.bfloat16)
-    returned_grads = lax.all_to_all(
-        grad_inputs, "expert", split_axis=1, concat_axis=0, tiled=True
-    ).reshape(experts * capacity, model_width)
+    returned_grads = pairwise_exchange(grad_inputs, "expert", 1, 0).reshape(
+        experts * capacity, model_width
+    )
     gathered_grads = jnp.take(returned_grads, flat_rows.reshape(-1), axis=0).reshape(
         token_count, fanout, model_width
     )

time: 1640 us -> 1770 us (1.079)
  waiting for transfers between devices: 912 us -> 1040 us
    all_to_all x1 -> x0, waiting for transfers between devices: 141 us -> none  [body(): lax.all_to_all(grad_inputs, 'expert', split_axis=1, concat_axis=0, tiled=...]
    ppermute x0 -> x3, waiting for transfers between devices: none -> 123 us  [pairwise_exchange(): lax.ppermute(sent, axis, [(i, i ^ step) for i in range(size)])]
    reduce_scatter x1, waiting for transfers between devices: 0.02 us -> 72 us  [body(): lax.psum_scatter(grad_expert_in.astype(jnp.bfloat16), 'dp', scatter_dimen...]
    reduce_scatter x1, waiting for transfers between devices: 0.01 us -> 48.9 us  [body(): lax.psum_scatter(grad_expert_out.astype(jnp.bfloat16), 'dp', scatter_dime...]
    unnamed x8, waiting for transfers between devices: 107 us -> 134 us
  transfers between devices with their start and end apart: 9 -> 11, of which waited for: 6 -> 9; matrix products, arithmetic and copies ran while one was open for 14% -> 11% of each run, Pallas kernels for 0% -> 0%
where the time goes in v1:
time: 1770 us; the launch traced here: 1760 us
  waiting for transfers between devices  1040 us (59%)
  local copies, waits for them, and re-layouts  251 us (14%)
  blocking collectives  189 us (11%)
  matrix products  164 us (9%)
  other arithmetic  81.9 us (5%)
    all_to_all x1, blocking collectives, body(): lax.all_to_all(outgoing, 'expert', split_axis=0, concat_axis=1, tiled=True)  189 us
    all_to_all x1, waiting for transfers between devices, body(): lax.all_to_all(outgoing_grads.reshape(experts, capacity, model_width), 'e...  182 us
    reduce_scatter x1, waiting for transfers between devices, body(): lax.psum_scatter(grad_heads_in, ('dp', 'expert'), scatter_dimension=0, ti...  181 us
    all_to_all x1, waiting for transfers between devices, body(): lax.all_to_all(result, 'expert', split_axis=1, concat_axis=0, tiled=True)  152 us
    reduce_scatter x1, waiting for transfers between devices, body(): lax.psum_scatter(grad_heads_out, ('dp', 'expert'), scatter_dimension=0, t...  146 us
    unnamed x8, waiting for transfers between devices  134 us
    ppermute x3, waiting for transfers between devices, pairwise_exchange(): lax.ppermute(sent, axis, [(i, i ^ step) for i in range(size)])  123 us
    reduce_scatter x1, waiting for transfers between devices, body(): lax.psum_scatter(grad_expert_in.astype(jnp.bfloat16), 'dp', scatter_dimen...  72 us
  transfers between devices with their start and end apart: 11, of which 9 were waited for; matrix products, arithmetic and copies ran while one was open for 11% of the time, Pallas kernels for 0%

profile of v1, /device:TPU:0, one launch (start us, length us, event | category | flops | bytes accessed | tf_op | source)
XLA Modules:
  0.0 1757.7 jit_solution(8017710401255701486)
XLA Ops:
  9.5 4.3 fusion.56
  17.6 3.0 copy.178
  20.6 2.6 slice_negate_fusion.1
  29.9 2.3 fusion.33
  33.9 1.9 exponential_reduce_fusion
  37.5 2.4 convolution_convert_fusion.5
  39.9 2.2 multiply_reduce_fusion.2
  44.6 25.3 %gather_fusion.1 = f32[3072]{0:T(1024)S(1)} fusion(f32[384,16]{0,1:T(8,128)S(1)} %fusion.100, s32[3072]{0:T(1024)S(1)} %reshape.438), kind=kCustom, calls=%fused_computation.5 | custom fusion | bytes 49152 | tf_op jit(solution)/shard_map/jit(take_along_axis)/gather | solution.py:174
  72.1 20.2 %gather_fusion.2 = s32[3072]{0:T(1024)S(1)} fusion(s32[384,16]{1,0:T(8,128)S(1)} %bitcast_subtract_fusion.1, s32[3072]{0:T(1024)S(1)} %reshape.438), kind=kCustom, calls=%fused_computation.6 | custom fusion | bytes 49152 | tf_op jit(solution)/shard_map/jit(take_along_axis)/gather | solution.py:181
  93.6 11.8 scatter_custom_fusion
  105.5 18.3 %gather_fusion.5 = bf16[4096,1024]{1,0:T(8,128)(2,1)} fusion(bf16[384,1024]{1,0:T(8,128)(2,1)S(1)} %multiply_convert_fusion.4, s32[4096]{0:T(1024)S(1)} %fusion.65), kind=kCustom, calls=%fused_computation.clone | custom fusion | bytes 16793600 | tf_op jit(solution)/shard_map/jit(_take)/gather | solution.py:197
  123.7 4.4 broadcast_select_fusion
  128.2 189.2 %all_to_all.51 = bf16[16,256,1024]{2,1,0:T(8,128)(2,1)} all-to-all(bf16[16,256,1024]{2,1,0:T(8,128)(2,1)S(1)} %bitcast.184), channel_id=1, replica_groups=mesh['dp'=8,'expert'=4] {'expert'}, dimensions={0} | all-to-all | bytes 16777216 | tf_op jit(solution)/shard_map/all_to_all | solution.py:200
  317.4 8.0 copy.192
  325.4 17.0 fusion.101
  342.4 8.5 multiply_convert_fusion.3
  351.0 11.6 convolution_convert_fusion.2
  362.6 12.3 copy.195
  374.9 5.7 all-to-all-start.1
  380.8 18.2 %gather_fusion.7 = bf16[4096,1024]{1,0:T(8,128)(2,1)} fusion(bf16[384,1024]{1,0:T(8,128)(2,1)S(1)} %copy-done.3, s32[4096]{0:T(1024)S(1)} %fusion.65), kind=kCustom, calls=%fused_computation.2.clone | custom fusion | bytes 16793600 | tf_op jit(solution)/shard_map/jit(_take)/gather | solution.py:217
  399.0 11.8 scatter_custom_fusion.1
  410.9 152.0 %all-to-all-done.1 = bf16[4,1024,1024]{2,0,1:T(4,128)(2,1)} async-done(((bf16[4,1024,1024]{2,0,1:T(4,128)(2,1)}), bf16[4,1024,1024]{2,0,1:T(4,128)(2,1)}, u32[]{:S(2)}, u32[]{:S(2)}) %all-to-all-start.1) | async-done | bytes 8388640 | tf_op jit(solution)/shard_map/all_to_all | solution.py:208
  562.8 9.8 copy.196
  572.6 20.4 %gather_fusion.6 = bf16[3072,1024]{1,0:T(8,128)(2,1)} fusion(bf16[4096,1024]{1,0:T(8,128)(2,1)} %bitcast.179, s32[3072]{0:T(1024)S(1)} %fusion.72), kind=kCustom, calls=%fused_computation.1.clone | custom fusion | bytes 12595200 | tf_op jit(solution)/shard_map/jit(_take)/gather | solution.py:211
  593.0 6.4 fusion.7
  599.8 23.0 %gather_fusion = f32[4096]{0:T(1024)S(1)} fusion(f32[3072]{0:T(1024)S(1)} %div.58, s32[4096]{0:T(1024)S(1)} %fusion.64), kind=kCustom, calls=%fused_computation.4 | custom fusion | bytes 49152 | tf_op jit(solution)/shard_map/jit(_take)/gather | solution.py:193
  622.8 7.8 multiply_convert_fusion
  630.7 5.6 all-to-all-start.2
  636.5 182.3 %all-to-all-done.2 = bf16[16,256,1024]{2,1,0:T(8,128)(2,1)} async-done(((bf16[16,256,1024]{2,1,0:T(8,128)(2,1)}), bf16[16,256,1024]{2,1,0:T(8,128)(2,1)}, u32[]{:S(2)}, u32[]{:S(2)}) %all-to-all-start.2) | async-done | bytes 8388640 | tf_op jit(solution)/shard_map/all_to_all | solution.py:219
  818.8 8.0 copy.198
  826.8 15.2 multiply_convert_fusion.2
  842.1 16.4 convolution_convert_fusion.1
  858.5 7.1 dynamic-slice_bitcast_fusion.3
  865.6 2.0 collective-permute-start.1
  867.7 2.4 collective-permute-start.2
  872.1 12.2 convert_reduce_fusion.1
  884.3 75.0 %collective-permute-done = bf16[4,256,1024]{2,1,0:T(8,128)(2,1)} collective-permute-done((bf16[4,256,1024]{2,1,0:T(8,128)(2,1)}, bf16[4,256,1024]{2,1,0:T(8,128)(2,1)}, u32[]{:S(2)}, u32[]{:S(2)}) %collective-permute-start) | collective-permute-done | bytes 2097184 | tf_op jit(solution)/shard_map/ppermute | solution.py:36
  959.2 48.2 %collective-permute-done.1 = bf16[4,256,1024]{2,1,0:T(8,128)(2,1)} collective-permute-done((bf16[4,256,1024]{2,1,0:T(8,128)(2,1)}, bf16[4,256,1024]{2,1,0:T(8,128)(2,1)}, u32[]{:S(2)}, u32[]{:S(2)}) %collective-permute-start.1) | collective-permute-done | bytes 2097184 | tf_op jit(solution)/shard_map/ppermute | solution.py:36
  1007.4 3.9 pad_maximum_fusion.1
  1011.3 3.8 fusion.96
  1015.1 5.0 gather_fusion.3
  1020.1 5.0 gather_fusion.4
  1025.1 8.0 pad_maximum_fusion.2
  1033.1 20.4 %gather_fusion.8 = bf16[3072,1024]{1,0:T(8,128)(2,1)} fusion(bf16[4096,1024]{1,0:T(8,128)(2,1)} %bitcast.178, s32[3072]{0:T(1024)S(1)} %fusion.72), kind=kCustom, calls=%fused_computation.3.clone | custom fusion | bytes 12595200 | tf_op jit(solution)/shard_map/jit(_take)/gather | solution.py:248
  1053.5 7.1 convert_reduce_fusion
  1066.7 2.3 copy.201
  1069.0 10.5 fusion
  1079.6 3.1 fusion.37
  1082.7 11.2 fusion.2
  1093.9 3.4 convolution_multiply_fusion
  1101.5 3.2 fusion.30
  1105.9 11.7 convolution_convert_fusion.3
  1117.6 4.9 fusion.48
  1122.7 16.7 convolution_convert_fusion
  1139.4 7.1 fusion.44
  1148.0 3.4 fusion.29
  1151.4 134.3 %reduce-scatter.19.cloned.1.call-done = f32[32,2]{1,0:T(8,128)} async-done(((f32[1024,2]{1,0:T(8,128)}), f32[32,2]{1,0:T(8,128)}) %reduce-scatter.19.cloned.1.call-update) | async-done | bytes 272
  1287.8 48.9 %reduce-scatter.17.cloned.1.call-done = bf16[4,128,512]{2,1,0:T(8,128)(2,1)} async-done(((bf16[4,1024,512]{2,1,0:T(8,128)(2,1)}), bf16[4,128,512]{2,1,0:T(8,128)(2,1)}) %reduce-scatter.17.cloned.1.call-update) | async-done | bytes 524304 | tf_op jit(solution)/shard_map/reduce_scatter | solution.py:320
  1336.7 4.1 multiply_add_fusion.2
  1340.8 146.0 %reduce-scatter.13.cloned.1.call-done = f32[32,1024]{1,0:T(8,128)} async-done(((f32[1024,1024]{1,0:T(8,128)}), f32[32,1024]{1,0:T(8,128)}) %reduce-scatter.13.cloned.1.call-update) | async-done | bytes 131088 | tf_op jit(solution)/shard_map/reduce_scatter | solution.py:312
  1488.5 72.0 %reduce-scatter.15.cloned.1.call-done = bf16[4,128,1024]{2,1,0:T(8,128)(2,1)} async-done(((bf16[4,1024,1024]{2,1,0:T(8,128)(2,1)}), bf16[4,128,1024]{2,1,0:T(8,128)(2,1)}) %reduce-scatter.15.cloned.1.call-update) | async-done | bytes 1048592 | tf_op jit(solution)/shard_map/reduce_scatter | solution.py:317
  1560.5 6.9 multiply_add_fusion
  1567.5 181.0 %reduce-scatter.11.cloned.1.call-done = f32[32,2048]{1,0:T(8,128)} async-done(((f32[1024,2048]{1,0:T(8,128)}), f32[32,2048]{1,0:T(8,128)}) %reduce-scatter.11.cloned.1.call-update) | async-done | bytes 262160 | tf_op jit(solution)/shard_map/reduce_scatter | solution.py:311
  1748.5 1.9 multiply_add_fusion.3
  (239 shorter events, 41.2 us)
Async XLA Ops:
  7.2 32.7 %copy-start = (bf16[1024,1024]{1,0:T(8,128)(2,1)S(1)}, bf16[1024,1024]{1,0:T(8,128)(2,1)}, u32[]{:S(2)}) copy-start(bf16[1024,1024]{1,0:T(8,128)(2,1)} %param.42) | copy-start | bytes 6291460
  8.1 5.7 copy-start.35
  8.1 34.3 %copy-start.47 = (f32[1024,1]{0,1:T(1,128)}, f32[1024,1]{0,1:T(1,128)S(1)}, u32[]{:S(2)}) copy-start(f32[1024,1]{0,1:T(1,128)S(1)} %get-tuple-element.72) | copy-start | bytes 12292
  9.5 4.3 copy-start.49
  13.8 2.3 copy-start.30
  15.1 8.1 copy-start.60
  24.4 7.8 copy-start.19
  24.4 7.8 copy-start.22
  28.6 7.2 copy-start.15
  29.9 3.9 copy-start.13
  33.8 3.6 copy-start.5
  33.9 3.6 copy-start.24
  35.8 4.1 copy-start.37
  37.5 2.4 copy-start.9
  39.9 2.2 copy-start.26
  39.9 4.4 copy-start.41
  44.3 61.1 %copy-start.1 = (bf16[384,1024]{1,0:T(8,128)(2,1)}, bf16[384,1024]{1,0:T(8,128)(2,1)S(1)}, u32[]{:S(2)}) copy-start(bf16[384,1024]{1,0:T(8,128)(2,1)S(1)} %multiply_convert_fusion.4) | copy-start | bytes 2359300
  44.6 26.1 %copy-start.46 = (s32[16,3,128]{2,0,1:T(8,128)S(1)}, s32[16,3,128]{2,0,1:T(8,128)}, u32[]{:S(2)}) copy-start(s32[16,3,128]{2,0,1:T(8,128)} %copy_bitcast_fusion) | copy-start | bytes 73732
  44.6 27.5 %copy-start.25 = (s32[384,16]{1,0:T(8,128)S(1)}, s32[384,16]{1,0:T(8,128)}, u32[]{:S(2)}) copy-start(s32[384,16]{1,0:T(8,128)} %copy.188) | copy-start | bytes 73732
  374.9 5.8 copy-start.3
  374.9 187.9 %all-to-all-start.1 = ((bf16[4,1024,1024]{2,0,1:T(4,128)(2,1)}), bf16[4,1024,1024]{2,0,1:T(4,128)(2,1)}, u32[]{:S(2)}, u32[]{:S(2)}) async-start(bf16[4,1024,1024]{2,0,1:T(4,128)(2,1)} %copy.195), calls=%async_computation.1 | async-start | bytes 16777216 | tf_op jit(solution)/shard_map/all_to_all | solution.py:208
  380.7 30.0 %copy-start.40 = (f32[384,8]{0,1:T(8,128)S(1)}, f32[384,8]{0,1:T(8,128)}, u32[]{:S(2)}) copy-start(f32[384,8]{0,1:T(8,128)} %copy-done.39) | copy-start | bytes 36868
  380.7 30.0 %copy-start.54 = (f32[384]{0:T(512)S(1)}, f32[384]{0:T(512)}, u32[]{:S(2)}) copy-start(f32[384]{0:T(512)} %get-tuple-element.46) | copy-start | bytes 4612
  630.7 188.1 %all-to-all-start.2 = ((bf16[16,256,1024]{2,1,0:T(8,128)(2,1)}), bf16[16,256,1024]{2,1,0:T(8,128)(2,1)}, u32[]{:S(2)}, u32[]{:S(2)}) async-start(bf16[16,256,1024]{2,1,0:T(8,128)(2,1)} %bitcast.185), calls=%async_computation.2 | async-start | bytes 16777216 | tf_op jit(solution)/shard_map/all_to_all | solution.py:219
  636.2 510.3 %reduce-scatter.21.cloned.1.call-start = ((), (), s32[]{:S(2)}) async-start(), calls=%async_computation.14 | async-start | bytes 540672
  858.5 11.5 copy-start.51
  858.5 11.7 copy-start.31
  858.5 11.7 copy-start.2
  865.6 93.6 %collective-permute-start = (bf16[4,256,1024]{2,1,0:T(8,128)(2,1)}, bf16[4,256,1024]{2,1,0:T(8,128)(2,1)}, u32[]{:S(2)}, u32[]{:S(2)}) collective-permute-start(bf16[4,256,1024]{2,1,0:T(8,128)(2,1)} %get-tuple-element.55), channel_id=1, source_target_pairs={{0,1},{1,0},{2,3},{3,2},{4,5},{5,4},{6,7},{7,6},{8,9},{9,8},{10,11... | collective-permute-start | bytes 6291464 | tf_op jit(solution)/shard_map/ppermute | solution.py:36
  865.6 141.8 %collective-permute-start.1 = (bf16[4,256,1024]{2,1,0:T(8,128)(2,1)}, bf16[4,256,1024]{2,1,0:T(8,128)(2,1)}, u32[]{:S(2)}, u32[]{:S(2)}) collective-permute-start(bf16[4,256,1024]{2,1,0:T(8,128)(2,1)} %get-tuple-element.54), channel_id=1, source_target_pairs={{0,2},{1,3},{2,0},{3,1},{4,6},{5,7},{6,4},{7,5},{8,10},{9,11},{10,... | collective-permute-start | bytes 6291464 | tf_op jit(solution)/shard_map/ppermute | solution.py:36
  867.7 139.8 %collective-permute-start.2 = (bf16[4,256,1024]{2,1,0:T(8,128)(2,1)}, bf16[4,256,1024]{2,1,0:T(8,128)(2,1)}, u32[]{:S(2)}, u32[]{:S(2)}) collective-permute-start(bf16[4,256,1024]{2,1,0:T(8,128)(2,1)} %get-tuple-element.53), channel_id=1, source_target_pairs={{0,3},{1,2},{2,1},{3,0},{4,7},{5,6},{6,5},{7,4},{8,11},{9,10},{10,... | collective-permute-start | bytes 6291464 | tf_op jit(solution)/shard_map/ppermute | solution.py:36
  872.0 413.7 %reduce-scatter.19.cloned.1.call-start = ((), (), s32[]{:S(2)}) async-start(), calls=%async_computation.13 | async-start | bytes 540672
  872.1 135.3 %copy-start.8 = (bf16[1,4,256,1024]{3,2,1,0:T(8,128)(2,1)S(1)}, bf16[1,4,256,1024]{3,2,1,0:T(8,128)(2,1)}, u32[]{:S(2)}) copy-start(bf16[1,4,256,1024]{3,2,1,0:T(8,128)(2,1)} %get-tuple-element.52) | copy-start | bytes 6291460
  1053.5 7.1 copy-start.7
  1053.5 7.2 copy-start.42
  1053.5 7.2 copy-start.48
  1053.5 7.2 copy-start.53
  1064.8 4.2 copy-start.16
  1064.8 4.2 copy-start.38
  1064.9 14.7 slice-start
  1069.0 10.6 slice-start.1
  1069.0 10.6 slice-start.2
  1069.0 10.6 copy-start.17
  1082.7 11.2 copy-start.14
  1093.9 3.5 copy-start.20
  1093.9 4.6 slice-start.3
  1098.5 2.4 copy-start.18
  1098.9 2.0 copy-start.10
  1098.9 2.0 copy-start.29
  1098.9 2.0 copy-start.36
  1098.9 2.0 copy-start.50
  1099.0 2.6 copy-start.61
  1105.8 230.9 %reduce-scatter.17.cloned.1.call-start = ((), (), s32[]{:S(2)}) async-start(), calls=%async_computation.12 | async-start | bytes 4718592 | tf_op jit(solution)/shard_map/reduce_scatter | solution.py:320
  1117.6 369.2 %reduce-scatter.13.cloned.1.call-start = ((), (), s32[]{:S(2)}) async-start(), calls=%async_computation.10 | async-start | bytes 4325376 | tf_op jit(solution)/shard_map/reduce_scatter | solution.py:312
  1122.6 437.9 %reduce-scatter.15.cloned.1.call-start = ((), (), s32[]{:S(2)}) async-start(), calls=%async_computation.11 | async-start | bytes 9437184 | tf_op jit(solution)/shard_map/reduce_scatter | solution.py:317
  1139.4 609.1 %reduce-scatter.11.cloned.1.call-start = ((), (), s32[]{:S(2)}) async-start(), calls=%async_computation.9 | async-start | bytes 8650752 | tf_op jit(solution)/shard_map/reduce_scatter | solution.py:311
  1146.5 140.0 %copy-start.58 = (f32[32,2]{0,1:T(2,128)S(1)}, f32[32,2]{0,1:T(2,128)}, u32[]{:S(2)}) copy-start(f32[32,2]{0,1:T(2,128)} %param.37) | copy-start | bytes 772
  1146.5 140.0 %copy-start.59 = (f32[32,2]{0,1:T(2,128)S(1)}, f32[32,2]{0,1:T(2,128)}, u32[]{:S(2)}) copy-start(f32[32,2]{0,1:T(2,128)} %param.36) | copy-start | bytes 772
  1151.4 335.4 %copy-start.43 = (f32[32,1024]{1,0:T(8,128)S(1)}, f32[32,1024]{1,0:T(8,128)}, u32[]{:S(2)}) copy-start(f32[32,1024]{1,0:T(8,128)} %param.45) | copy-start | bytes 393220
  1151.4 335.4 %copy-start.44 = (f32[32,1024]{1,0:T(8,128)S(1)}, f32[32,1024]{1,0:T(8,128)}, u32[]{:S(2)}) copy-start(f32[32,1024]{1,0:T(8,128)} %param.43) | copy-start | bytes 393220
  1151.4 335.4 %copy-start.45 = (f32[32,1024]{1,0:T(8,128)S(1)}, f32[32,1024]{1,0:T(8,128)}, u32[]{:S(2)}) copy-start(f32[32,1024]{1,0:T(8,128)} %param.44) | copy-start | bytes 393220
  1488.5 260.0 %copy-start.32 = (f32[32,2048]{1,0:T(8,128)S(1)}, f32[32,2048]{1,0:T(8,128)}, u32[]{:S(2)}) copy-start(f32[32,2048]{1,0:T(8,128)} %param.41) | copy-start | bytes 786436
  1488.5 260.0 %copy-start.33 = (f32[32,2048]{1,0:T(8,128)S(1)}, f32[32,2048]{1,0:T(8,128)}, u32[]{:S(2)}) copy-start(f32[32,2048]{1,0:T(8,128)} %param.39) | copy-start | bytes 786436
  1488.5 260.0 %copy-start.34 = (f32[32,2048]{1,0:T(8,128)S(1)}, f32[32,2048]{1,0:T(8,128)}, u32[]{:S(2)}) copy-start(f32[32,2048]{1,0:T(8,128)} %param.40) | copy-start | bytes 786436
  (14 other events, 16.9 us)
Sparse Core Ops, SparseCore 0:
  872.2 237.9 reduce-scatter.20
  1113.1 172.5 reduce-scatter.18
  1289.1 47.6 reduce-scatter.16
  1339.0 147.7 reduce-scatter.12
  1490.5 69.9 reduce-scatter.14
  1562.7 185.7 reduce-scatter.10
